TPU v7x, 32 devices: a whole 2x2x4 slice. The times are simulated.
32 devices in a mesh: lat: 16 (over z, x, core), lon: 2 (over y).
Axes of the slice: x: 2, y: 2, z: 4, core: 2. Of those that a mesh axis runs over, the one named last changes fastest.
Arguments:
- state: bfloat16 [2, 96, 128, 256], P(None, 'lat', 'lon'), may hold values from -6 to 6
- upstream: bfloat16 [2, 96, 128, 256], P(None, 'lat', 'lon'), may hold values from -6 to 6
- first_kernel: bfloat16 [9, 256, 256], replicated, may hold values from -0.125 to 0.125
- second_kernel: bfloat16 [9, 256, 256], replicated, may hold values from -0.125 to 0.125
Outputs:
- output_state: bfloat16 [2, 96, 128, 256], P(None, 'lat', 'lon')
- state_grad: bfloat16 [2, 96, 128, 256], P(None, 'lat', 'lon')
- first_grad: float32 [9, 256, 256], P(None, 'lat', 'lon')
- second_grad: float32 [9, 256, 256], P(None, 'lat', 'lon')
All inputs are finite; a program needn't handle non-finite values.
Results may differ from a plain program's by a relative error of at most 0.0033.
Values may be sent and summed in bfloat16 or wider, within the bound.
A program may use at most 64 MiB of HBM per device.

v0:
```python
import math
import jax
import jax.numpy as jnp
from jax import lax
from jax.sharding import PartitionSpec as P


def with_halo(array, sides, width, wrap):
    for axis, dim in sides:
        size, length = (lax.axis_size(axis), array.shape[dim])
        up = [(i, (i + 1) % size) for i in range(size if wrap else size - 1)]
        down = [(j, i) for i, j in up]
        last = lax.slice_in_dim(array, length - width, length, axis=dim)
        leading = lax.slice_in_dim(array, 0, width, axis=dim)
        before = lax.ppermute(last, axis, up)
        after = lax.ppermute(leading, axis, down)
        array = jnp.concatenate([before, array, after], axis=dim)
    return array


def pad_cycle(stacked):
    wide = with_halo(stacked, (("lon", 3),), 1, True)
    return with_halo(wide, (("lat", 2),), 1, False)


def conv_taps(padded, kernel, flipped):
    band_rows = padded.shape[1] - 2
    band_cols = padded.shape[2] - 2
    total = jnp.zeros((padded.shape[0], band_rows, band_cols, kernel.shape[2]), jnp.float32)
    for row_off in range(3):
        for col_off in range(3):
            window = padded[:, row_off : row_off + band_rows, col_off : col_off + band_cols, :]
            if flipped:
                total = total + jnp.einsum(
                    "bijd,cd->bijc",
                    window,
                    kernel[8 - 3 * row_off - col_off],
                    preferred_element_type=jnp.float32,
                )
            else:
                total = total + jnp.einsum(
                    "bijc,cd->bijd",
                    window,
                    kernel[3 * row_off + col_off],
                    preferred_element_type=jnp.float32,
                )
    return total


def kernel_terms(padded, grad_field):
    band_rows = grad_field.shape[1]
    band_cols = grad_field.shape[2]
    result = []
    for row_off in range(3):
        for col_off in range(3):
            window = padded[:, row_off : row_off + band_rows, col_off : col_off + band_cols, :]
            result.append(
                jnp.einsum("bijc,bijd->cd", window, grad_field, preferred_element_type=jnp.float32)
            )
    return jnp.stack(result)


def sum_lat(terms):
    moved = (
        lax.all_to_all(terms[0][None], "lat", split_axis=2, concat_axis=0, tiled=True),
        lax.all_to_all(terms[1][None], "lat", split_axis=2, concat_axis=0, tiled=True),
    )
    return (jnp.sum(moved[0], axis=0), jnp.sum(moved[1], axis=0))


def sum_lon(terms):
    moved = (
        lax.all_to_all(terms[0][None], "lon", split_axis=3, concat_axis=0, tiled=True),
        lax.all_to_all(terms[1][None], "lon", split_axis=3, concat_axis=0, tiled=True),
    )
    return (jnp.sum(moved[0], axis=0), jnp.sum(moved[1], axis=0))


def body(state, upstream, first_kernel, second_kernel):
    band_rows = state.shape[1]
    band_cols = state.shape[2]
    scale_factor = 1.0 / math.sqrt(
        band_rows * lax.axis_size("lat") * band_cols * lax.axis_size("lon")
    )
    both_pad = pad_cycle(jnp.stack([state, upstream]))
    state_pad = both_pad[0]
    upstream_pad = both_pad[1]
    pre = conv_taps(state_pad, first_kernel, False)
    active = jax.nn.silu(pre).astype(jnp.bfloat16)
    active_pad = pad_cycle(active[None])[0]
    second_out = conv_taps(active_pad, second_kernel, False)
    output_state = (state.astype(jnp.float32) + second_out).astype(jnp.bfloat16)
    back_act = conv_taps(upstream_pad, second_kernel, True)
    sigma = jax.nn.sigmoid(pre)
    back_pre = (back_act * sigma * (1.0 + pre * (1.0 - sigma))).astype(jnp.bfloat16)
    back_pad = pad_cycle(back_pre[None])[0]
    state_grad = (upstream.astype(jnp.float32) + conv_taps(back_pad, first_kernel, True)).astype(
        jnp.bfloat16
    )
    terms = (
        kernel_terms(state_pad, back_pre) * scale_factor,
        kernel_terms(active_pad, upstream) * scale_factor,
    )
    summed = sum_lon(sum_lat(terms))
    return (output_state, state_grad, summed[0], summed[1])


def solution(mesh):
    placed = (P(None, "lat", "lon", None), P(None, "lat", "lon", None), P(), P())
    return jax.shard_map(
        body,
        mesh=mesh,
        in_specs=placed,
        out_specs=(
            P(None, "lat", "lon", None),
            P(None, "lat", "lon", None),
            P(None, "lat", "lon"),
            P(None, "lat", "lon"),
        ),
        check_vma=False,
    )
```

profile of v0, /device:TPU:20, one launch (start us, length us, event | category | flops | bytes accessed | tf_op | source)
XLA Modules:
  0.0 192.8 jit_solution(8814331763132578597)
XLA Ops:
  0.7 1.0 pad_maximum_fusion.12
  2.2 1.5 collective-permute-start
  3.7 1.8 collective-permute-done.1
  6.0 1.0 pad_maximum_fusion.4
  7.1 1.9 collective-permute-start.3
  9.0 2.4 %collective-permute-start.2 = (bf16[2,2,1,66,256]{4,3,2,1,0:T(8,128)(2,1)S(1)}, bf16[2,2,1,66,256]{4,3,2,1,0:T(8,128)(2,1)S(1)}, u32[]{:S(2)}, u32[]{:S(2)}) collective-permute-start(bf16[2,2,1,66,256]{4,3,2,1,0:T(8,128)(2,1)S(1)} %get-tuple-element.14), channel_id=1, source_target_pairs={{0,2},{2,4},{4,6},{6,8},{8,10},{10,12},{12,14},{14,16},{16,18},{18... | collective-permute-start | bytes 405512 | tf_op jit(solution)/shard_map/ppermute | solution.py:15
  11.7 4.7 %collective-permute-done.2 = bf16[2,2,1,66,256]{4,3,2,1,0:T(8,128)(2,1)S(1)} collective-permute-done((bf16[2,2,1,66,256]{4,3,2,1,0:T(8,128)(2,1)S(1)}, bf16[2,2,1,66,256]{4,3,2,1,0:T(8,128)(2,1)S(1)}, u32[]{:S(2)}, u32[]{:S(2)}) %collective-permute-start.2) | collective-permute-done | bytes 135200 | tf_op jit(solution)/shard_map/ppermute | solution.py:15
  17.0 1.2 copy-done.4
  20.6 1.0 copy-done.6
  27.7 3.9 %copy.16 = f32[1,9,256,256]{3,0,1,2:T(1,128)} copy(f32[1,9,256,256]{3,2,1,0:T(8,128)S(1)} %broadcast_multiply_fusion.1) | data formatting | bytes 4718592 | tf_op jit(solution)/shard_map/mul | solution.py:101
  31.6 5.3 %all-to-all-start = ((f32[1,9,256,256]{3,0,1,2:T(1,128)}), f32[1,9,256,256]{3,0,1,2:T(1,128)S(1)}, u32[]{:S(2)}, u32[]{:S(2)}) async-start(f32[1,9,256,256]{3,0,1,2:T(1,128)} %copy.16), calls=%async_computation | async-start | bytes 4718592 | tf_op jit(solution)/shard_map/all_to_all | solution.py:65
  37.1 1.6 collective-permute-start.5
  39.2 1.6 collective-permute-start.9
  41.3 1.1 collective-permute-done.4
  42.4 2.0 %collective-permute-start.7 = (bf16[1,2,1,66,256]{4,3,2,1,0:T(8,128)(2,1)S(1)}, bf16[1,2,1,66,256]{4,3,2,1,0:T(8,128)(2,1)S(1)}, u32[]{:S(2)}, u32[]{:S(2)}) collective-permute-start(bf16[1,2,1,66,256]{4,3,2,1,0:T(8,128)(2,1)S(1)} %get-tuple-element.21), channel_id=1, source_target_pairs={{2,0},{4,2},{6,4},{8,6},{10,8},{12,10},{14,12},{16,14},{18,16},{20... | collective-permute-start | bytes 202760 | tf_op jit(solution)/shard_map/ppermute | solution.py:16
  44.4 2.4 %collective-permute-start.6 = (bf16[1,2,1,66,256]{4,3,2,1,0:T(8,128)(2,1)S(1)}, bf16[1,2,1,66,256]{4,3,2,1,0:T(8,128)(2,1)S(1)}, u32[]{:S(2)}, u32[]{:S(2)}) collective-permute-start(bf16[1,2,1,66,256]{4,3,2,1,0:T(8,128)(2,1)S(1)} %get-tuple-element.20), channel_id=1, source_target_pairs={{0,2},{2,4},{4,6},{6,8},{8,10},{10,12},{12,14},{14,16},{16,18},{18... | collective-permute-start | bytes 202760 | tf_op jit(solution)/shard_map/ppermute | solution.py:15
  47.5 4.1 %collective-permute-start.11 = (bf16[1,2,1,66,256]{4,3,2,1,0:T(8,128)(2,1)}, bf16[1,2,1,66,256]{4,3,2,1,0:T(8,128)(2,1)S(1)}, u32[]{:S(2)}, u32[]{:S(2)}) collective-permute-start(bf16[1,2,1,66,256]{4,3,2,1,0:T(8,128)(2,1)} %get-tuple-element.19), channel_id=1, source_target_pairs={{2,0},{4,2},{6,4},{8,6},{10,8},{12,10},{14,12},{16,14},{18,16},{20... | collective-permute-start | bytes 202760 | tf_op jit(solution)/shard_map/ppermute | solution.py:16
  51.6 2.1 %collective-permute-start.10 = (bf16[1,2,1,66,256]{4,3,2,1,0:T(8,128)(2,1)S(1)}, bf16[1,2,1,66,256]{4,3,2,1,0:T(8,128)(2,1)}, u32[]{:S(2)}, u32[]{:S(2)}) collective-permute-start(bf16[1,2,1,66,256]{4,3,2,1,0:T(8,128)(2,1)S(1)} %get-tuple-element.18), channel_id=1, source_target_pairs={{0,2},{2,4},{4,6},{6,8},{8,10},{10,12},{12,14},{14,16},{16,18},{18... | collective-permute-start | bytes 202760 | tf_op jit(solution)/shard_map/ppermute | solution.py:15
  53.7 35.3 %collective-permute-done.7 = bf16[1,2,1,66,256]{4,3,2,1,0:T(8,128)(2,1)S(1)} collective-permute-done((bf16[1,2,1,66,256]{4,3,2,1,0:T(8,128)(2,1)S(1)}, bf16[1,2,1,66,256]{4,3,2,1,0:T(8,128)(2,1)S(1)}, u32[]{:S(2)}, u32[]{:S(2)}) %collective-permute-start.7) | collective-permute-done | bytes 67616 | tf_op jit(solution)/shard_map/ppermute | solution.py:16
  89.0 1.9 collective-permute-done.6
  94.2 3.9 %copy.22 = f32[1,9,256,256]{3,0,1,2:T(1,128)} copy(f32[1,9,256,256]{3,2,1,0:T(8,128)S(1)} %broadcast_multiply_fusion) | data formatting | bytes 4718592 | tf_op jit(solution)/shard_map/mul | solution.py:102
  98.1 4.3 %all-to-all-start.2 = ((f32[1,9,256,256]{3,0,1,2:T(1,128)}), f32[1,9,256,256]{3,0,1,2:T(1,128)}, u32[]{:S(2)}, u32[]{:S(2)}) async-start(f32[1,9,256,256]{3,0,1,2:T(1,128)} %copy.22), calls=%async_computation.2 | async-start | bytes 4718592 | tf_op jit(solution)/shard_map/all_to_all | solution.py:66
  103.1 1.2 maximum_bitcast_fusion.1
  104.3 1.3 fusion.61
  107.8 0.7 copy-done.1
  108.6 1.0 fusion.4
  111.1 1.2 convolution_add_fusion.2
  112.3 2.5 %copy.66 = f32[1,9,256,256]{3,1,2,0:T(8,128)} copy(f32[1,9,256,256]{3,0,1,2:T(1,128)S(1)} %all-to-all-done) | data formatting | bytes 4718592 | tf_op jit(solution)/shard_map/all_to_all | solution.py:65
  114.8 2.7 %reduce_sum.36 = f32[9,16,256]{2,0,1:T(8,128)S(1)} reduce(f32[9,16,16,256]{3,0,2,1:T(8,128)} %bitcast.349, f32[]{:T(128)} %constant.2.clone.1), dimensions={1}, to_apply=%region_0.1 | reduce | flops 552960 | bytes 2506756 | tf_op jit(solution)/shard_map/reduce_sum | solution.py:68
  117.5 2.1 %copy.19 = f32[1,9,16,256]{2,0,1,3:T(1,128)} copy(f32[1,9,16,256]{3,1,2,0:T(8,128)S(1)} %bitcast.366) | data formatting | bytes 294912 | tf_op jit(solution)/shard_map/broadcast_in_dim | solution.py:73
  120.2 4.9 %reduce.12 = f32[256,9,16]{2,1,0:T(8,128)S(1)} reduce(f32[256,9,1,16]{3,2,1,0:T(1,128)} %bitcast.361, f32[]{:T(128)} %broadcast.23), dimensions={2}, to_apply=%bitcast.327.reduce_sub_computation | reduce | bytes 294916
  125.1 1.1 reshape.308
  126.2 29.4 %all-to-all-done.2 = f32[1,9,256,256]{3,0,1,2:T(1,128)} async-done(((f32[1,9,256,256]{3,0,1,2:T(1,128)}), f32[1,9,256,256]{3,0,1,2:T(1,128)}, u32[]{:S(2)}, u32[]{:S(2)}) %all-to-all-start.2) | async-done | bytes 2359328 | tf_op jit(solution)/shard_map/all_to_all | solution.py:66
  155.7 4.9 %all-to-all-start.1 = ((f32[2,1,18432]{2,1,0:T(1,128)}), f32[2,1,18432]{2,1,0:T(1,128)S(1)}, u32[]{:S(2)}, u32[]{:S(2)}) async-start(f32[2,1,18432]{2,1,0:T(1,128)} %reshape.308), calls=%async_computation.1 | async-start | bytes 294912 | tf_op jit(solution)/shard_map/all_to_all | solution.py:73
  160.6 2.4 %convolution_add_fusion.1 = f32[2,6,64,256]{3,2,1,0:T(8,128)} fusion(f32[2,6,64,256]{3,2,1,0:T(8,128)} %convolution_add_fusion.2, bf16[2,8,66,256]{3,2,1,0:T(8,128)(2,1)S(1)} %maximum_bitcast_fusion.1, bf16[9,256,256]{2,1,0:T(8,128)(2,1)} %param.6), kind=kOutput, calls=%fused_computation.2 | convolution fusion | flops 100859904 | bytes 2097152 | tf_op jit(solution)/shard_map/bijd,cd->bijc/dot_general | solution.py:34
  163.0 4.2 %copy.67 = f32[1,9,256,256]{3,1,2,0:T(8,128)} copy(f32[1,9,256,256]{3,0,1,2:T(1,128)} %all-to-all-done.2) | data formatting | bytes 4718592 | tf_op jit(solution)/shard_map/all_to_all | solution.py:66
  167.2 2.7 %reduce_sum.38 = f32[9,16,256]{2,0,1:T(8,128)S(1)} reduce(f32[9,16,16,256]{3,0,2,1:T(8,128)} %bitcast.350, f32[]{:T(128)} %constant.2.clone.1), dimensions={1}, to_apply=%region_2.3 | reduce | flops 552960 | bytes 2506756 | tf_op jit(solution)/shard_map/reduce_sum | solution.py:68
  169.9 2.1 %copy.25 = f32[1,9,16,256]{2,0,1,3:T(1,128)} copy(f32[1,9,16,256]{3,1,2,0:T(8,128)S(1)} %bitcast.367) | data formatting | bytes 294912 | tf_op jit(solution)/shard_map/broadcast_in_dim | solution.py:74
  172.0 4.9 %reduce.14 = f32[256,9,16]{2,1,0:T(8,128)S(1)} reduce(f32[256,9,1,16]{3,2,1,0:T(1,128)} %bitcast.362, f32[]{:T(128)} %broadcast.23), dimensions={2}, to_apply=%bitcast.329.reduce_sub_computation | reduce | bytes 294916
  177.0 1.1 reshape.310
  178.1 3.7 %all-to-all-start.3 = ((f32[2,1,18432]{2,1,0:T(1,128)}), f32[2,1,18432]{2,1,0:T(1,128)S(1)}, u32[]{:S(2)}, u32[]{:S(2)}) async-start(f32[2,1,18432]{2,1,0:T(1,128)} %reshape.310), calls=%async_computation.3 | async-start | bytes 294912 | tf_op jit(solution)/shard_map/all_to_all | solution.py:74
  181.8 2.3 %fusion.6 = bf16[2,6,64,256]{3,2,1,0:T(8,128)(2,1)} fusion(f32[2,6,64,256]{3,2,1,0:T(8,128)} %convolution_add_fusion.1, bf16[2,6,64,256]{3,2,1,0:T(8,128)(2,1)S(1)} %copy-done.3, bf16[2,8,66,256]{3,2,1,0:T(8,128)(2,1)S(1)} %maximum_bitcast_fusion.1, bf16[9,256,256]{2,1,0:T(8,128)(2,1)} %param.6), kind=kOutput, calls=%fused_computation.38 | convolution fusion | flops 101449728 | bytes 2097152 | tf_op jit(solution)/shard_map/bijd,cd->bijc/dot_general | solution.py:34
  184.0 1.1 reduce.13
  185.1 1.9 reshape.309
  187.5 0.9 copy.28
  188.4 1.1 reduce.15
  189.5 1.9 reshape.311
  191.8 0.9 copy.29
  (98 shorter events, 21.2 us)
Async XLA Ops:
  0.6 15.7 %copy-start.2 = (bf16[2,6,64,256]{3,2,1,0:T(8,128)(2,1)S(1)}, bf16[2,6,64,256]{3,2,1,0:T(8,128)(2,1)}, u32[]{:S(2)}) copy-start(bf16[2,6,64,256]{3,2,1,0:T(8,128)(2,1)} %param.5) | copy-start | bytes 1179652
  0.6 15.7 %copy-start = (bf16[2,6,64,256]{3,2,1,0:T(8,128)(2,1)S(1)}, bf16[2,6,64,256]{3,2,1,0:T(8,128)(2,1)}, u32[]{:S(2)}) copy-start(bf16[2,6,64,256]{3,2,1,0:T(8,128)(2,1)} %param.4) | copy-start | bytes 1179652
  1.6 3.9 %collective-permute-start.1 = (bf16[2,2,6,1,256]{4,3,2,1,0:T(2,128)(2,1)S(1)}, bf16[2,2,6,1,256]{4,3,2,1,0:T(2,128)(2,1)S(1)}, u32[]{:S(2)}, u32[]{:S(2)}) collective-permute-start(bf16[2,2,6,1,256]{4,3,2,1,0:T(2,128)(2,1)S(1)} %get-tuple-element.17), channel_id=1, source_target_pairs={{1,0},{0,1},{3,2},{2,3},{5,4},{4,5},{7,6},{6,7},{9,8},{8,9},{11,10... | collective-permute-start | bytes 36872 | tf_op jit(solution)/shard_map/ppermute | solution.py:16
  2.2 3.8 %collective-permute-start = (bf16[2,2,6,1,256]{4,3,2,1,0:T(2,128)(2,1)S(1)}, bf16[2,2,6,1,256]{4,3,2,1,0:T(2,128)(2,1)S(1)}, u32[]{:S(2)}, u32[]{:S(2)}) collective-permute-start(bf16[2,2,6,1,256]{4,3,2,1,0:T(2,128)(2,1)S(1)} %get-tuple-element.16), channel_id=1, source_target_pairs={{0,1},{1,0},{2,3},{3,2},{4,5},{5,4},{6,7},{7,6},{8,9},{9,8},{10,11... | collective-permute-start | bytes 36872 | tf_op jit(solution)/shard_map/ppermute | solution.py:15
  7.1 4.6 %collective-permute-start.3 = (bf16[2,2,1,66,256]{4,3,2,1,0:T(8,128)(2,1)S(1)}, bf16[2,2,1,66,256]{4,3,2,1,0:T(8,128)(2,1)S(1)}, u32[]{:S(2)}, u32[]{:S(2)}) collective-permute-start(bf16[2,2,1,66,256]{4,3,2,1,0:T(8,128)(2,1)S(1)} %get-tuple-element.15), channel_id=1, source_target_pairs={{2,0},{4,2},{6,4},{8,6},{10,8},{12,10},{14,12},{16,14},{18,16},{20... | collective-permute-start | bytes 405512 | tf_op jit(solution)/shard_map/ppermute | solution.py:16
  9.0 7.4 %collective-permute-start.2 = (bf16[2,2,1,66,256]{4,3,2,1,0:T(8,128)(2,1)S(1)}, bf16[2,2,1,66,256]{4,3,2,1,0:T(8,128)(2,1)S(1)}, u32[]{:S(2)}, u32[]{:S(2)}) collective-permute-start(bf16[2,2,1,66,256]{4,3,2,1,0:T(8,128)(2,1)S(1)} %get-tuple-element.14), channel_id=1, source_target_pairs={{0,2},{2,4},{4,6},{6,8},{8,10},{10,12},{12,14},{14,16},{16,18},{18... | collective-permute-start | bytes 405512 | tf_op jit(solution)/shard_map/ppermute | solution.py:15
  16.9 1.3 copy-start.4
  20.4 1.3 copy-start.6
  24.6 2.6 %copy-start.8 = (bf16[2,6,64,256]{3,2,1,0:T(8,128)(2,1)}, bf16[2,6,64,256]{3,2,1,0:T(8,128)(2,1)S(1)}, u32[]{:S(2)}) copy-start(bf16[2,6,64,256]{3,2,1,0:T(8,128)(2,1)S(1)} %fusion.5) | copy-start | bytes 1179652
  31.6 66.5 %all-to-all-start = ((f32[1,9,256,256]{3,0,1,2:T(1,128)}), f32[1,9,256,256]{3,0,1,2:T(1,128)S(1)}, u32[]{:S(2)}, u32[]{:S(2)}) async-start(f32[1,9,256,256]{3,0,1,2:T(1,128)} %copy.16), calls=%async_computation | async-start | bytes 4718592 | tf_op jit(solution)/shard_map/all_to_all | solution.py:65
  36.8 2.4 %copy-start.9 = (bf16[2,6,64,256]{3,2,1,0:T(8,128)(2,1)S(1)}, bf16[2,6,64,256]{3,2,1,0:T(8,128)(2,1)}, u32[]{:S(2)}) copy-start(bf16[2,6,64,256]{3,2,1,0:T(8,128)(2,1)} %copy-done.8) | copy-start | bytes 1179652
  37.1 4.2 %collective-permute-start.5 = (bf16[1,2,6,1,256]{4,3,2,1,0:T(2,128)(2,1)S(1)}, bf16[1,2,6,1,256]{4,3,2,1,0:T(2,128)(2,1)S(1)}, u32[]{:S(2)}, u32[]{:S(2)}) collective-permute-start(bf16[1,2,6,1,256]{4,3,2,1,0:T(2,128)(2,1)S(1)} %get-tuple-element.25), channel_id=1, source_target_pairs={{1,0},{0,1},{3,2},{2,3},{5,4},{4,5},{7,6},{6,7},{9,8},{8,9},{11,10... | collective-permute-start | bytes 18440 | tf_op jit(solution)/shard_map/ppermute | solution.py:16
  38.7 3.7 %collective-permute-start.4 = (bf16[1,2,6,1,256]{4,3,2,1,0:T(2,128)(2,1)S(1)}, bf16[1,2,6,1,256]{4,3,2,1,0:T(2,128)(2,1)S(1)}, u32[]{:S(2)}, u32[]{:S(2)}) collective-permute-start(bf16[1,2,6,1,256]{4,3,2,1,0:T(2,128)(2,1)S(1)} %get-tuple-element.24), channel_id=1, source_target_pairs={{0,1},{1,0},{2,3},{3,2},{4,5},{5,4},{6,7},{7,6},{8,9},{9,8},{10,11... | collective-permute-start | bytes 18440 | tf_op jit(solution)/shard_map/ppermute | solution.py:15
  39.2 7.6 %collective-permute-start.9 = (bf16[1,2,6,1,256]{4,3,2,1,0:T(2,128)(2,1)S(1)}, bf16[1,2,6,1,256]{4,3,2,1,0:T(2,128)(2,1)S(1)}, u32[]{:S(2)}, u32[]{:S(2)}) collective-permute-start(bf16[1,2,6,1,256]{4,3,2,1,0:T(2,128)(2,1)S(1)} %get-tuple-element.23), channel_id=1, source_target_pairs={{1,0},{0,1},{3,2},{2,3},{5,4},{4,5},{7,6},{6,7},{9,8},{8,9},{11,10... | collective-permute-start | bytes 18440 | tf_op jit(solution)/shard_map/ppermute | solution.py:16
  40.8 6.0 %collective-permute-start.8 = (bf16[1,2,6,1,256]{4,3,2,1,0:T(2,128)(2,1)S(1)}, bf16[1,2,6,1,256]{4,3,2,1,0:T(2,128)(2,1)S(1)}, u32[]{:S(2)}, u32[]{:S(2)}) collective-permute-start(bf16[1,2,6,1,256]{4,3,2,1,0:T(2,128)(2,1)S(1)} %get-tuple-element.22), channel_id=1, source_target_pairs={{0,1},{1,0},{2,3},{3,2},{4,5},{5,4},{6,7},{7,6},{8,9},{9,8},{10,11... | collective-permute-start | bytes 18440 | tf_op jit(solution)/shard_map/ppermute | solution.py:15
  42.4 46.6 %collective-permute-start.7 = (bf16[1,2,1,66,256]{4,3,2,1,0:T(8,128)(2,1)S(1)}, bf16[1,2,1,66,256]{4,3,2,1,0:T(8,128)(2,1)S(1)}, u32[]{:S(2)}, u32[]{:S(2)}) collective-permute-start(bf16[1,2,1,66,256]{4,3,2,1,0:T(8,128)(2,1)S(1)} %get-tuple-element.21), channel_id=1, source_target_pairs={{2,0},{4,2},{6,4},{8,6},{10,8},{12,10},{14,12},{16,14},{18,16},{20... | collective-permute-start | bytes 202760 | tf_op jit(solution)/shard_map/ppermute | solution.py:16
  44.4 46.5 %collective-permute-start.6 = (bf16[1,2,1,66,256]{4,3,2,1,0:T(8,128)(2,1)S(1)}, bf16[1,2,1,66,256]{4,3,2,1,0:T(8,128)(2,1)S(1)}, u32[]{:S(2)}, u32[]{:S(2)}) collective-permute-start(bf16[1,2,1,66,256]{4,3,2,1,0:T(8,128)(2,1)S(1)} %get-tuple-element.20), channel_id=1, source_target_pairs={{0,2},{2,4},{4,6},{6,8},{8,10},{10,12},{12,14},{14,16},{16,18},{18... | collective-permute-start | bytes 202760 | tf_op jit(solution)/shard_map/ppermute | solution.py:15
  46.8 0.7 copy-start.11
  47.5 55.0 %collective-permute-start.11 = (bf16[1,2,1,66,256]{4,3,2,1,0:T(8,128)(2,1)}, bf16[1,2,1,66,256]{4,3,2,1,0:T(8,128)(2,1)S(1)}, u32[]{:S(2)}, u32[]{:S(2)}) collective-permute-start(bf16[1,2,1,66,256]{4,3,2,1,0:T(8,128)(2,1)} %get-tuple-element.19), channel_id=1, source_target_pairs={{2,0},{4,2},{6,4},{8,6},{10,8},{12,10},{14,12},{16,14},{18,16},{20... | collective-permute-start | bytes 202760 | tf_op jit(solution)/shard_map/ppermute | solution.py:16
  51.6 51.5 %collective-permute-start.10 = (bf16[1,2,1,66,256]{4,3,2,1,0:T(8,128)(2,1)S(1)}, bf16[1,2,1,66,256]{4,3,2,1,0:T(8,128)(2,1)}, u32[]{:S(2)}, u32[]{:S(2)}) collective-permute-start(bf16[1,2,1,66,256]{4,3,2,1,0:T(8,128)(2,1)S(1)} %get-tuple-element.18), channel_id=1, source_target_pairs={{0,2},{2,4},{4,6},{6,8},{8,10},{10,12},{12,14},{14,16},{16,18},{18... | collective-permute-start | bytes 202760 | tf_op jit(solution)/shard_map/ppermute | solution.py:15
  98.1 57.6 %all-to-all-start.2 = ((f32[1,9,256,256]{3,0,1,2:T(1,128)}), f32[1,9,256,256]{3,0,1,2:T(1,128)}, u32[]{:S(2)}, u32[]{:S(2)}) async-start(f32[1,9,256,256]{3,0,1,2:T(1,128)} %copy.22), calls=%async_computation.2 | async-start | bytes 4718592 | tf_op jit(solution)/shard_map/all_to_all | solution.py:66
  102.4 3.2 %copy-start.5 = (bf16[9,256,256]{2,1,0:T(8,128)(2,1)S(1)}, bf16[9,256,256]{2,1,0:T(8,128)(2,1)}, u32[]{:S(2)}) copy-start(bf16[9,256,256]{2,1,0:T(8,128)(2,1)} %param.6) | copy-start | bytes 3538948
  102.4 0.6 copy-start.10
  104.3 1.6 copy-start.7
  107.6 1.0 copy-start.1
  155.7 22.4 %all-to-all-start.1 = ((f32[2,1,18432]{2,1,0:T(1,128)}), f32[2,1,18432]{2,1,0:T(1,128)S(1)}, u32[]{:S(2)}, u32[]{:S(2)}) async-start(f32[2,1,18432]{2,1,0:T(1,128)} %reshape.308), calls=%async_computation.1 | async-start | bytes 294912 | tf_op jit(solution)/shard_map/all_to_all | solution.py:73
  177.0 4.8 %copy-start.3 = (bf16[2,6,64,256]{3,2,1,0:T(8,128)(2,1)S(1)}, bf16[2,6,64,256]{3,2,1,0:T(8,128)(2,1)}, u32[]{:S(2)}) copy-start(bf16[2,6,64,256]{3,2,1,0:T(8,128)(2,1)} %param.5) | copy-start | bytes 1179652
  178.1 10.3 %all-to-all-start.3 = ((f32[2,1,18432]{2,1,0:T(1,128)}), f32[2,1,18432]{2,1,0:T(1,128)S(1)}, u32[]{:S(2)}, u32[]{:S(2)}) async-start(f32[2,1,18432]{2,1,0:T(1,128)} %reshape.310), calls=%async_computation.3 | async-start | bytes 294912 | tf_op jit(solution)/shard_map/all_to_all | solution.py:74
where the time goes:
time: 194 us; the launch traced here: 193 us
  waiting for transfers between devices  74.9 us (39%)
  starting transfers between devices  39.3 us (20%)
  local copies, waits for them, and re-layouts  31.2 us (16%)
  other arithmetic  23.3 us (12%)
  matrix products  22.7 us (12%)
    ppermute x6, waiting for transfers between devices, with_halo(): after = lax.ppermute(leading, axis, down)  37.4 us
    all_to_all x1, waiting for transfers between devices, sum_lat(): lax.all_to_all(terms[1][None], 'lat', split_axis=2, concat_axis=0, tiled=...  29.4 us
    unnamed x33, local copies, waits for them, and re-layouts  12.3 us
    ppermute x6, starting transfers between devices, with_halo(): after = lax.ppermute(leading, axis, down)  11.8 us
    dot_general x18, matrix products, conv_taps(): jnp.einsum('bijd,cd->bijc', window, kernel[8 - 3 * row_off - col_off], pr...  10.5 us
    unnamed x2, other arithmetic  9.8 us
    ppermute x6, starting transfers between devices, with_halo(): before = lax.ppermute(last, axis, up)  9.37 us
    ppermute x6, waiting for transfers between devices, with_halo(): before = lax.ppermute(last, axis, up)  8.16 us
  transfers between devices with their start and end apart: 16, of which 8 were waited for; matrix products, arithmetic and copies ran while one was open for 28% of the time, Pallas kernels for 0%

commit v1 on v0

--- a/solution.py
+++ b/solution.py
@@ -63,7 +63,12 @@
 def sum_lat(terms):
     moved = (
         lax.all_to_all(terms[0][None], "lat", split_axis=2, concat_axis=0, tiled=True),
-        lax.all_to_all(terms[1][None], "lat", split_axis=2, concat_axis=0, tiled=True),
+        jnp.concatenate(
+            lax.all_to_all(
+                jnp.stack(jnp.split(terms[1][None], lax.axis_size("lat"), axis=2)), "lat", 0, 0
+            ),
+            axis=0,
+        ),
     )
     return (jnp.sum(moved[0], axis=0), jnp.sum(moved[1], axis=0))
 

time: 194 us -> 203 us (1.046)
  other arithmetic: 23.3 us -> 27.4 us
  starting transfers between devices: 39.3 us -> 42 us
  waiting for transfers between devices: 74.9 us -> 77.6 us
    unnamed x33 -> x48, local copies, waits for them, and re-layouts: 12.3 us -> 19.9 us
    all_to_all x1 -> x0, local copies, waits for them, and re-layouts: 4.2 us -> none  [sum_lat(): lax.all_to_all(terms[1][None], 'lat', split_axis=2, concat_axis=0, tiled=...]
    mul x1 -> x0, local copies, waits for them, and re-layouts: 3.91 us -> none  [body(): kernel_terms(active_pad, upstream) * scale_factor]
    ppermute x6, waiting for transfers between devices: 37.4 us -> 40.9 us  [with_halo(): after = lax.ppermute(leading, axis, down)]
  transfers between devices with their start and end apart: 16 -> 16, of which waited for: 8 -> 7; matrix products, arithmetic and copies ran while one was open for 28% -> 34% of each run, Pallas kernels for 0% -> 0%
where the time goes in v1:
time: 203 us; the launch traced here: 202 us
  waiting for transfers between devices  77.6 us (38%)
  starting transfers between devices  42 us (21%)
  local copies, waits for them, and re-layouts  31.3 us (15%)
  other arithmetic  27.4 us (13%)
  matrix products  22.4 us (11%)
    ppermute x6, waiting for transfers between devices, with_halo(): after = lax.ppermute(leading, axis, down)  40.9 us
    all_to_all x1, waiting for transfers between devices, sum_lat(): lax.all_to_all(jnp.stack(jnp.split(terms[1][None], lax.axis_size('lat'),...  29.6 us
    unnamed x48, local copies, waits for them, and re-layouts  19.9 us
    ppermute x6, starting transfers between devices, with_halo(): after = lax.ppermute(leading, axis, down)  13.4 us
    dot_general x18, matrix products, conv_taps(): jnp.einsum('bijd,cd->bijc', window, kernel[8 - 3 * row_off - col_off], pr...  10.3 us
    unnamed x2, other arithmetic  9.93 us
    ppermute x6, starting transfers between devices, with_halo(): before = lax.ppermute(last, axis, up)  8.98 us
    ppermute x6, waiting for transfers between devices, with_halo(): before = lax.ppermute(last, axis, up)  7.04 us
  transfers between devices with their start and end apart: 16, of which 7 were waited for; matrix products, arithmetic and copies ran while one was open for 34% of the time, Pallas kernels for 0%

profile of v1, /device:TPU:20, one launch (start us, length us, event | category | flops | bytes accessed | tf_op | source)
XLA Modules:
  0.0 201.9 jit_solution(8849661104267004494)
XLA Ops:
  0.6 0.9 pad_maximum_fusion.12
  2.1 1.5 collective-permute-start
  3.6 1.8 collective-permute-done.1
  6.0 1.0 pad_maximum_fusion.4
  7.0 2.1 %collective-permute-start.3 = (bf16[2,2,1,66,256]{4,3,2,1,0:T(8,128)(2,1)S(1)}, bf16[2,2,1,66,256]{4,3,2,1,0:T(8,128)(2,1)S(1)}, u32[]{:S(2)}, u32[]{:S(2)}) collective-permute-start(bf16[2,2,1,66,256]{4,3,2,1,0:T(8,128)(2,1)S(1)} %get-tuple-element.15), channel_id=1, source_target_pairs={{2,0},{4,2},{6,4},{8,6},{10,8},{12,10},{14,12},{16,14},{18,16},{20... | collective-permute-start | bytes 405512 | tf_op jit(solution)/shard_map/ppermute | solution.py:16
  9.1 2.4 %collective-permute-start.2 = (bf16[2,2,1,66,256]{4,3,2,1,0:T(8,128)(2,1)S(1)}, bf16[2,2,1,66,256]{4,3,2,1,0:T(8,128)(2,1)S(1)}, u32[]{:S(2)}, u32[]{:S(2)}) collective-permute-start(bf16[2,2,1,66,256]{4,3,2,1,0:T(8,128)(2,1)S(1)} %get-tuple-element.14), channel_id=1, source_target_pairs={{0,2},{2,4},{4,6},{6,8},{8,10},{10,12},{12,14},{14,16},{16,18},{18... | collective-permute-start | bytes 405512 | tf_op jit(solution)/shard_map/ppermute | solution.py:15
  11.7 4.7 %collective-permute-done.2 = bf16[2,2,1,66,256]{4,3,2,1,0:T(8,128)(2,1)S(1)} collective-permute-done((bf16[2,2,1,66,256]{4,3,2,1,0:T(8,128)(2,1)S(1)}, bf16[2,2,1,66,256]{4,3,2,1,0:T(8,128)(2,1)S(1)}, u32[]{:S(2)}, u32[]{:S(2)}) %collective-permute-start.2) | collective-permute-done | bytes 135200 | tf_op jit(solution)/shard_map/ppermute | solution.py:15
  16.4 1.7 pad_maximum_fusion
  21.0 1.6 collective-permute-start.5
  26.4 1.6 collective-permute-start.9
  31.3 3.9 %copy.14 = f32[1,9,256,256]{3,0,1,2:T(1,128)} copy(f32[1,9,256,256]{3,2,1,0:T(8,128)S(1)} %broadcast_multiply_fusion.1) | data formatting | bytes 4718592 | tf_op jit(solution)/shard_map/mul | solution.py:106
  35.2 5.4 %all-to-all-start = ((f32[1,9,256,256]{3,0,1,2:T(1,128)}), f32[1,9,256,256]{3,0,1,2:T(1,128)S(1)}, u32[]{:S(2)}, u32[]{:S(2)}) async-start(f32[1,9,256,256]{3,0,1,2:T(1,128)} %copy.14), calls=%async_computation | async-start | bytes 4718592 | tf_op jit(solution)/shard_map/all_to_all | solution.py:65
  40.6 3.1 %collective-permute-start.7 = (bf16[1,2,1,66,256]{4,3,2,1,0:T(8,128)(2,1)S(1)}, bf16[1,2,1,66,256]{4,3,2,1,0:T(8,128)(2,1)S(1)}, u32[]{:S(2)}, u32[]{:S(2)}) collective-permute-start(bf16[1,2,1,66,256]{4,3,2,1,0:T(8,128)(2,1)S(1)} %get-tuple-element.21), channel_id=1, source_target_pairs={{2,0},{4,2},{6,4},{8,6},{10,8},{12,10},{14,12},{16,14},{18,16},{20... | collective-permute-start | bytes 202760 | tf_op jit(solution)/shard_map/ppermute | solution.py:16
  43.7 1.9 collective-permute-start.6
  45.7 1.6 pad_maximum_fusion.7
  47.3 4.5 %collective-permute-start.11 = (bf16[1,2,1,66,256]{4,3,2,1,0:T(8,128)(2,1)}, bf16[1,2,1,66,256]{4,3,2,1,0:T(8,128)(2,1)S(1)}, u32[]{:S(2)}, u32[]{:S(2)}) collective-permute-start(bf16[1,2,1,66,256]{4,3,2,1,0:T(8,128)(2,1)} %get-tuple-element.19), channel_id=1, source_target_pairs={{2,0},{4,2},{6,4},{8,6},{10,8},{12,10},{14,12},{16,14},{18,16},{20... | collective-permute-start | bytes 202760 | tf_op jit(solution)/shard_map/ppermute | solution.py:16
  51.8 2.1 %collective-permute-start.10 = (bf16[1,2,1,66,256]{4,3,2,1,0:T(8,128)(2,1)S(1)}, bf16[1,2,1,66,256]{4,3,2,1,0:T(8,128)(2,1)}, u32[]{:S(2)}, u32[]{:S(2)}) collective-permute-start(bf16[1,2,1,66,256]{4,3,2,1,0:T(8,128)(2,1)S(1)} %get-tuple-element.18), channel_id=1, source_target_pairs={{0,2},{2,4},{4,6},{6,8},{8,10},{10,12},{12,14},{14,16},{16,18},{18... | collective-permute-start | bytes 202760 | tf_op jit(solution)/shard_map/ppermute | solution.py:15
  53.9 38.9 %collective-permute-done.7 = bf16[1,2,1,66,256]{4,3,2,1,0:T(8,128)(2,1)S(1)} collective-permute-done((bf16[1,2,1,66,256]{4,3,2,1,0:T(8,128)(2,1)S(1)}, bf16[1,2,1,66,256]{4,3,2,1,0:T(8,128)(2,1)S(1)}, u32[]{:S(2)}, u32[]{:S(2)}) %collective-permute-start.7) | collective-permute-done | bytes 67616 | tf_op jit(solution)/shard_map/ppermute | solution.py:16
  92.8 1.8 collective-permute-done.6
  94.6 1.2 maximum_bitcast_fusion
  100.8 0.7 fusion.96
  105.5 0.7 fusion.89
  108.2 0.7 fusion.85
  109.5 4.3 %all-to-all-start.2 = ((f32[16,1,9,16,256]{4,3,2,1,0:T(8,128)}), f32[16,1,9,16,256]{4,3,2,1,0:T(8,128)}, u32[]{:S(2)}, u32[]{:S(2)}) async-start(f32[16,1,9,16,256]{4,3,2,1,0:T(8,128)} %fusion.84), calls=%async_computation.2 | async-start | bytes 4718592 | tf_op jit(solution)/shard_map/all_to_all | solution.py:67
  114.6 1.3 maximum_bitcast_fusion.1
  115.8 1.2 fusion.61
  119.7 1.0 fusion.4
  122.3 1.2 convolution_add_fusion.2
  123.5 2.5 %copy.61 = f32[1,9,256,256]{3,1,2,0:T(8,128)} copy(f32[1,9,256,256]{3,0,1,2:T(1,128)S(1)} %all-to-all-done) | data formatting | bytes 4718592 | tf_op jit(solution)/shard_map/all_to_all | solution.py:65
  126.0 2.7 %reduce_sum.36 = f32[9,16,256]{2,0,1:T(8,128)S(1)} reduce(f32[9,16,16,256]{3,0,2,1:T(8,128)} %bitcast.411, f32[]{:T(128)} %constant.2.clone.1), dimensions={1}, to_apply=%region_0.1 | reduce | flops 552960 | bytes 2506756 | tf_op jit(solution)/shard_map/reduce_sum | solution.py:73
  128.7 2.1 %copy.17 = f32[1,9,16,256]{2,0,1,3:T(1,128)} copy(f32[1,9,16,256]{3,1,2,0:T(8,128)S(1)} %bitcast.427) | data formatting | bytes 294912 | tf_op jit(solution)/shard_map/broadcast_in_dim | solution.py:78
  131.4 5.0 %reduce.10 = f32[256,9,16]{2,1,0:T(8,128)S(1)} reduce(f32[256,9,1,16]{3,2,1,0:T(1,128)} %bitcast.422, f32[]{:T(128)} %broadcast.23), dimensions={2}, to_apply=%bitcast.389.reduce_sub_computation | reduce | bytes 294916
  136.4 1.1 reshape.308
  137.5 29.6 %all-to-all-done.2 = f32[16,1,9,16,256]{4,3,2,1,0:T(8,128)} async-done(((f32[16,1,9,16,256]{4,3,2,1,0:T(8,128)}), f32[16,1,9,16,256]{4,3,2,1,0:T(8,128)}, u32[]{:S(2)}, u32[]{:S(2)}) %all-to-all-start.2) | async-done | bytes 2359328 | tf_op jit(solution)/shard_map/all_to_all | solution.py:67
  167.1 5.6 %all-to-all-start.1 = ((f32[2,1,18432]{2,1,0:T(1,128)}), f32[2,1,18432]{2,1,0:T(1,128)}, u32[]{:S(2)}, u32[]{:S(2)}) async-start(f32[2,1,18432]{2,1,0:T(1,128)} %reshape.308), calls=%async_computation.1 | async-start | bytes 294912 | tf_op jit(solution)/shard_map/all_to_all | solution.py:78
  172.7 2.1 %convolution_add_fusion.1 = f32[2,6,64,256]{3,2,1,0:T(8,128)} fusion(f32[2,6,64,256]{3,2,1,0:T(8,128)S(1)} %copy-done.8, bf16[2,8,66,256]{3,2,1,0:T(8,128)(2,1)S(1)} %maximum_bitcast_fusion.1, bf16[9,256,256]{2,1,0:T(8,128)(2,1)} %param.6), kind=kOutput, calls=%fused_computation.2 | convolution fusion | flops 100859904 | bytes 2097152 | tf_op jit(solution)/shard_map/bijd,cd->bijc/dot_general | solution.py:34
  174.8 1.9 reduce_sum.38
  176.7 2.1 %copy.20 = f32[1,9,16,256]{2,0,1,3:T(1,128)} copy(f32[1,9,16,256]{3,2,1,0:T(8,128)S(1)} %bitcast.428) | data formatting | bytes 294912 | tf_op jit(solution)/shard_map/broadcast_in_dim | solution.py:79
  178.8 5.0 %reduce.12 = f32[256,9,16]{2,1,0:T(8,128)S(1)} reduce(f32[256,9,1,16]{3,2,1,0:T(1,128)} %bitcast.423, f32[]{:T(128)} %broadcast.23), dimensions={2}, to_apply=%bitcast.391.reduce_sub_computation | reduce | bytes 294916
  183.7 1.1 reshape.310
  184.9 4.3 %all-to-all-start.3 = ((f32[2,1,18432]{2,1,0:T(1,128)}), f32[2,1,18432]{2,1,0:T(1,128)}, u32[]{:S(2)}, u32[]{:S(2)}) async-start(f32[2,1,18432]{2,1,0:T(1,128)} %reshape.310), calls=%async_computation.3 | async-start | bytes 294912 | tf_op jit(solution)/shard_map/all_to_all | solution.py:79
  189.1 2.3 %fusion.6 = bf16[2,6,64,256]{3,2,1,0:T(8,128)(2,1)} fusion(f32[2,6,64,256]{3,2,1,0:T(8,128)} %convolution_add_fusion.1, bf16[2,6,64,256]{3,2,1,0:T(8,128)(2,1)S(1)} %copy-done.2, bf16[2,8,66,256]{3,2,1,0:T(8,128)(2,1)S(1)} %maximum_bitcast_fusion.1, bf16[9,256,256]{2,1,0:T(8,128)(2,1)} %param.6), kind=kOutput, calls=%fused_computation.38 | convolution fusion | flops 101449728 | bytes 2097152 | tf_op jit(solution)/shard_map/bijd,cd->bijc/dot_general | solution.py:34
  191.4 2.0 reduce.11
  193.4 1.9 reshape.309
  195.8 0.9 copy.23
  196.7 2.0 reduce.13
  198.7 1.9 reshape.311
  201.0 0.9 copy.24
  (112 shorter events, 29.0 us)
Async XLA Ops:
  1.6 3.9 %collective-permute-start.1 = (bf16[2,2,6,1,256]{4,3,2,1,0:T(2,128)(2,1)S(1)}, bf16[2,2,6,1,256]{4,3,2,1,0:T(2,128)(2,1)S(1)}, u32[]{:S(2)}, u32[]{:S(2)}) collective-permute-start(bf16[2,2,6,1,256]{4,3,2,1,0:T(2,128)(2,1)S(1)} %get-tuple-element.17), channel_id=1, source_target_pairs={{1,0},{0,1},{3,2},{2,3},{5,4},{4,5},{7,6},{6,7},{9,8},{8,9},{11,10... | collective-permute-start | bytes 36872 | tf_op jit(solution)/shard_map/ppermute | solution.py:16
  2.1 3.8 %collective-permute-start = (bf16[2,2,6,1,256]{4,3,2,1,0:T(2,128)(2,1)S(1)}, bf16[2,2,6,1,256]{4,3,2,1,0:T(2,128)(2,1)S(1)}, u32[]{:S(2)}, u32[]{:S(2)}) collective-permute-start(bf16[2,2,6,1,256]{4,3,2,1,0:T(2,128)(2,1)S(1)} %get-tuple-element.16), channel_id=1, source_target_pairs={{0,1},{1,0},{2,3},{3,2},{4,5},{5,4},{6,7},{7,6},{8,9},{9,8},{10,11... | collective-permute-start | bytes 36872 | tf_op jit(solution)/shard_map/ppermute | solution.py:15
  7.0 11.2 %copy-start.3 = (bf16[9,256,256]{2,1,0:T(8,128)(2,1)S(1)}, bf16[9,256,256]{2,1,0:T(8,128)(2,1)}, u32[]{:S(2)}) copy-start(bf16[9,256,256]{2,1,0:T(8,128)(2,1)} %param.6) | copy-start | bytes 3538948
  7.0 4.7 %collective-permute-start.3 = (bf16[2,2,1,66,256]{4,3,2,1,0:T(8,128)(2,1)S(1)}, bf16[2,2,1,66,256]{4,3,2,1,0:T(8,128)(2,1)S(1)}, u32[]{:S(2)}, u32[]{:S(2)}) collective-permute-start(bf16[2,2,1,66,256]{4,3,2,1,0:T(8,128)(2,1)S(1)} %get-tuple-element.15), channel_id=1, source_target_pairs={{2,0},{4,2},{6,4},{8,6},{10,8},{12,10},{14,12},{16,14},{18,16},{20... | collective-permute-start | bytes 405512 | tf_op jit(solution)/shard_map/ppermute | solution.py:16
  9.1 7.4 %collective-permute-start.2 = (bf16[2,2,1,66,256]{4,3,2,1,0:T(8,128)(2,1)S(1)}, bf16[2,2,1,66,256]{4,3,2,1,0:T(8,128)(2,1)S(1)}, u32[]{:S(2)}, u32[]{:S(2)}) collective-permute-start(bf16[2,2,1,66,256]{4,3,2,1,0:T(8,128)(2,1)S(1)} %get-tuple-element.14), channel_id=1, source_target_pairs={{0,2},{2,4},{4,6},{6,8},{8,10},{10,12},{12,14},{14,16},{16,18},{18... | collective-permute-start | bytes 405512 | tf_op jit(solution)/shard_map/ppermute | solution.py:15
  20.1 2.9 %copy-start.5 = (bf16[9,256,256]{2,1,0:T(8,128)(2,1)S(1)}, bf16[9,256,256]{2,1,0:T(8,128)(2,1)}, u32[]{:S(2)}) copy-start(bf16[9,256,256]{2,1,0:T(8,128)(2,1)} %param.7) | copy-start | bytes 3538948
  21.0 19.6 %copy-start.7 = (bf16[1,2,6,64,256]{4,3,2,1,0:T(8,128)(2,1)}, bf16[1,2,6,64,256]{4,3,2,1,0:T(8,128)(2,1)S(1)}, u32[]{:S(2)}) copy-start(bf16[1,2,6,64,256]{4,3,2,1,0:T(8,128)(2,1)S(1)} %fusion.45) | copy-start | bytes 1179652
  21.0 19.5 %collective-permute-start.5 = (bf16[1,2,6,1,256]{4,3,2,1,0:T(2,128)(2,1)S(1)}, bf16[1,2,6,1,256]{4,3,2,1,0:T(2,128)(2,1)S(1)}, u32[]{:S(2)}, u32[]{:S(2)}) collective-permute-start(bf16[1,2,6,1,256]{4,3,2,1,0:T(2,128)(2,1)S(1)} %get-tuple-element.25), channel_id=1, source_target_pairs={{1,0},{0,1},{3,2},{2,3},{5,4},{4,5},{7,6},{6,7},{9,8},{8,9},{11,10... | collective-permute-start | bytes 18440 | tf_op jit(solution)/shard_map/ppermute | solution.py:16
  22.6 18.0 %collective-permute-start.4 = (bf16[1,2,6,1,256]{4,3,2,1,0:T(2,128)(2,1)S(1)}, bf16[1,2,6,1,256]{4,3,2,1,0:T(2,128)(2,1)S(1)}, u32[]{:S(2)}, u32[]{:S(2)}) collective-permute-start(bf16[1,2,6,1,256]{4,3,2,1,0:T(2,128)(2,1)S(1)} %get-tuple-element.24), channel_id=1, source_target_pairs={{0,1},{1,0},{2,3},{3,2},{4,5},{5,4},{6,7},{7,6},{8,9},{9,8},{10,11... | collective-permute-start | bytes 18440 | tf_op jit(solution)/shard_map/ppermute | solution.py:15
  26.0 4.7 %copy-start.9 = (bf16[2,6,64,256]{3,2,1,0:T(8,128)(2,1)}, bf16[2,6,64,256]{3,2,1,0:T(8,128)(2,1)S(1)}, u32[]{:S(2)}) copy-start(bf16[2,6,64,256]{3,2,1,0:T(8,128)(2,1)S(1)} %fusion.5) | copy-start | bytes 1179652
  26.4 19.3 %collective-permute-start.9 = (bf16[1,2,6,1,256]{4,3,2,1,0:T(2,128)(2,1)S(1)}, bf16[1,2,6,1,256]{4,3,2,1,0:T(2,128)(2,1)S(1)}, u32[]{:S(2)}, u32[]{:S(2)}) collective-permute-start(bf16[1,2,6,1,256]{4,3,2,1,0:T(2,128)(2,1)S(1)} %get-tuple-element.23), channel_id=1, source_target_pairs={{1,0},{0,1},{3,2},{2,3},{5,4},{4,5},{7,6},{6,7},{9,8},{8,9},{11,10... | collective-permute-start | bytes 18440 | tf_op jit(solution)/shard_map/ppermute | solution.py:16
  28.0 17.7 %collective-permute-start.8 = (bf16[1,2,6,1,256]{4,3,2,1,0:T(2,128)(2,1)S(1)}, bf16[1,2,6,1,256]{4,3,2,1,0:T(2,128)(2,1)S(1)}, u32[]{:S(2)}, u32[]{:S(2)}) collective-permute-start(bf16[1,2,6,1,256]{4,3,2,1,0:T(2,128)(2,1)S(1)} %get-tuple-element.22), channel_id=1, source_target_pairs={{0,1},{1,0},{2,3},{3,2},{4,5},{5,4},{6,7},{7,6},{8,9},{9,8},{10,11... | collective-permute-start | bytes 18440 | tf_op jit(solution)/shard_map/ppermute | solution.py:15
  35.1 60.6 %copy-start.1 = (bf16[2,6,64,256]{3,2,1,0:T(8,128)(2,1)S(1)}, bf16[2,6,64,256]{3,2,1,0:T(8,128)(2,1)}, u32[]{:S(2)}) copy-start(bf16[2,6,64,256]{3,2,1,0:T(8,128)(2,1)} %param.5) | copy-start | bytes 1179652
  35.2 74.4 %all-to-all-start = ((f32[1,9,256,256]{3,0,1,2:T(1,128)}), f32[1,9,256,256]{3,0,1,2:T(1,128)S(1)}, u32[]{:S(2)}, u32[]{:S(2)}) async-start(f32[1,9,256,256]{3,0,1,2:T(1,128)} %copy.14), calls=%async_computation | async-start | bytes 4718592 | tf_op jit(solution)/shard_map/all_to_all | solution.py:65
  40.6 52.2 %collective-permute-start.7 = (bf16[1,2,1,66,256]{4,3,2,1,0:T(8,128)(2,1)S(1)}, bf16[1,2,1,66,256]{4,3,2,1,0:T(8,128)(2,1)S(1)}, u32[]{:S(2)}, u32[]{:S(2)}) collective-permute-start(bf16[1,2,1,66,256]{4,3,2,1,0:T(8,128)(2,1)S(1)} %get-tuple-element.21), channel_id=1, source_target_pairs={{2,0},{4,2},{6,4},{8,6},{10,8},{12,10},{14,12},{16,14},{18,16},{20... | collective-permute-start | bytes 202760 | tf_op jit(solution)/shard_map/ppermute | solution.py:16
  43.7 50.8 %collective-permute-start.6 = (bf16[1,2,1,66,256]{4,3,2,1,0:T(8,128)(2,1)S(1)}, bf16[1,2,1,66,256]{4,3,2,1,0:T(8,128)(2,1)S(1)}, u32[]{:S(2)}, u32[]{:S(2)}) collective-permute-start(bf16[1,2,1,66,256]{4,3,2,1,0:T(8,128)(2,1)S(1)} %get-tuple-element.20), channel_id=1, source_target_pairs={{0,2},{2,4},{4,6},{6,8},{8,10},{10,12},{12,14},{14,16},{16,18},{18... | collective-permute-start | bytes 202760 | tf_op jit(solution)/shard_map/ppermute | solution.py:15
  45.7 47.1 %copy-start.11 = (bf16[1,2,6,1,256]{4,3,2,1,0:T(2,128)(2,1)}, bf16[1,2,6,1,256]{4,3,2,1,0:T(2,128)(2,1)S(1)}, u32[]{:S(2)}) copy-start(bf16[1,2,6,1,256]{4,3,2,1,0:T(2,128)(2,1)S(1)} %collective-permute-done.8) | copy-start | bytes 18436
  47.3 66.6 %collective-permute-start.11 = (bf16[1,2,1,66,256]{4,3,2,1,0:T(8,128)(2,1)}, bf16[1,2,1,66,256]{4,3,2,1,0:T(8,128)(2,1)S(1)}, u32[]{:S(2)}, u32[]{:S(2)}) collective-permute-start(bf16[1,2,1,66,256]{4,3,2,1,0:T(8,128)(2,1)} %get-tuple-element.19), channel_id=1, source_target_pairs={{2,0},{4,2},{6,4},{8,6},{10,8},{12,10},{14,12},{16,14},{18,16},{20... | collective-permute-start | bytes 202760 | tf_op jit(solution)/shard_map/ppermute | solution.py:16
  51.8 62.8 %collective-permute-start.10 = (bf16[1,2,1,66,256]{4,3,2,1,0:T(8,128)(2,1)S(1)}, bf16[1,2,1,66,256]{4,3,2,1,0:T(8,128)(2,1)}, u32[]{:S(2)}, u32[]{:S(2)}) collective-permute-start(bf16[1,2,1,66,256]{4,3,2,1,0:T(8,128)(2,1)S(1)} %get-tuple-element.18), channel_id=1, source_target_pairs={{0,2},{2,4},{4,6},{6,8},{8,10},{10,12},{12,14},{14,16},{16,18},{18... | collective-permute-start | bytes 202760 | tf_op jit(solution)/shard_map/ppermute | solution.py:15
  109.5 57.6 %all-to-all-start.2 = ((f32[16,1,9,16,256]{4,3,2,1,0:T(8,128)}), f32[16,1,9,16,256]{4,3,2,1,0:T(8,128)}, u32[]{:S(2)}, u32[]{:S(2)}) async-start(f32[16,1,9,16,256]{4,3,2,1,0:T(8,128)} %fusion.84), calls=%async_computation.2 | async-start | bytes 4718592 | tf_op jit(solution)/shard_map/all_to_all | solution.py:67
  113.9 3.1 %copy-start.4 = (bf16[9,256,256]{2,1,0:T(8,128)(2,1)S(1)}, bf16[9,256,256]{2,1,0:T(8,128)(2,1)}, u32[]{:S(2)}) copy-start(bf16[9,256,256]{2,1,0:T(8,128)(2,1)} %param.6) | copy-start | bytes 3538948
  113.9 3.4 %copy-start.6 = (bf16[9,256,256]{2,1,0:T(8,128)(2,1)S(1)}, bf16[9,256,256]{2,1,0:T(8,128)(2,1)}, u32[]{:S(2)}) copy-start(bf16[9,256,256]{2,1,0:T(8,128)(2,1)} %param.7) | copy-start | bytes 3538948
  113.9 0.6 copy-start.10
  118.7 1.0 copy-start
  131.4 41.3 %copy-start.8 = (f32[2,6,64,256]{3,2,1,0:T(8,128)S(1)}, f32[2,6,64,256]{3,2,1,0:T(8,128)}, u32[]{:S(2)}) copy-start(f32[2,6,64,256]{3,2,1,0:T(8,128)} %convolution_add_fusion.2) | copy-start | bytes 2359300
  167.1 17.7 %all-to-all-start.1 = ((f32[2,1,18432]{2,1,0:T(1,128)}), f32[2,1,18432]{2,1,0:T(1,128)}, u32[]{:S(2)}, u32[]{:S(2)}) async-start(f32[2,1,18432]{2,1,0:T(1,128)} %reshape.308), calls=%async_computation.1 | async-start | bytes 294912 | tf_op jit(solution)/shard_map/all_to_all | solution.py:78
  178.8 10.4 %copy-start.2 = (bf16[2,6,64,256]{3,2,1,0:T(8,128)(2,1)S(1)}, bf16[2,6,64,256]{3,2,1,0:T(8,128)(2,1)}, u32[]{:S(2)}) copy-start(bf16[2,6,64,256]{3,2,1,0:T(8,128)(2,1)} %param.5) | copy-start | bytes 1179652
  184.9 11.8 %all-to-all-start.3 = ((f32[2,1,18432]{2,1,0:T(1,128)}), f32[2,1,18432]{2,1,0:T(1,128)}, u32[]{:S(2)}, u32[]{:S(2)}) async-start(f32[2,1,18432]{2,1,0:T(1,128)} %reshape.310), calls=%async_computation.3 | async-start | bytes 294912 | tf_op jit(solution)/shard_map/all_to_all | solution.py:79
